TPU v7x, 256 devices: a whole 4x4x8 slice. The times are simulated.
256 devices in a mesh: expert: 64 (over z, x, core), tensor: 4 (over y).
Axes of the slice: x: 4, y: 4, z: 8, core: 2. Of those that a mesh axis runs over, the one named last changes fastest.
Arguments:
- tokens: bfloat16 [2048, 4096], P('expert', 'tensor'), may hold values from -6 to 6
- cotangent: bfloat16 [2048, 4096], P('expert', 'tensor'), may hold values from -6 to 6
- routing: int32 [2048, 8], P('expert'), may hold values from 0 to 63, as said below
- gates: float32 [2048, 8], P('expert'), may hold values from 0.1 to 0.4
- w_in: bfloat16 [64, 4096, 1536], P('expert', None, 'tensor'), may hold values from -0.09375 to 0.09375
- w_out: bfloat16 [64, 1536, 4096], P('expert', 'tensor'), may hold values from -0.15625 to 0.15625
Outputs:
- mixed: bfloat16 [2048, 4096], P('expert', 'tensor')
- d_tokens: bfloat16 [2048, 4096], P('expert', 'tensor')
- d_w_in: bfloat16 [64, 4096, 1536], P('expert', None, 'tensor')
- d_w_out: bfloat16 [64, 1536, 4096], P('expert', 'tensor')
Inputs may be any that keep to these rules, and one draw needn't show every extreme that they name: `routing`: each row names 8 different experts. In each aligned block of 32 rows (the tokens of one index of the expert axis) no expert is named by more than 8 rows, and one expert is named by exactly 8 rows of every block.
All inputs are finite; a program needn't handle non-finite values.
Results may differ from a plain program's by a relative error of at most 0.0058.
Values may be sent and summed in bfloat16 or wider, within the bound.
A program may use at most 128 MiB of HBM per device.

v0:
```python
import jax
import jax.numpy as jnp
from jax import lax
from jax.sharding import PartitionSpec as P


def shards(tokens, cotangent, routing, gates, w_in, w_out):
    devices = lax.axis_size("expert")
    local_experts = w_in.shape[0]
    experts = devices * local_experts
    tok_rows = routing.shape[0]
    capacity = tok_rows // 4
    buffer_rows = experts * capacity
    highest = lax.Precision.HIGHEST
    matches = (routing[:, :, None] == jnp.arange(experts, dtype=jnp.int32)[None, None, :]).astype(
        jnp.int32
    )
    per_token = jnp.sum(matches, axis=1)
    earlier = jnp.cumsum(per_token, axis=0) - per_token
    destination = routing * capacity + jnp.take_along_axis(earlier, routing, axis=1)
    placed = (
        destination[:, :, None] == jnp.arange(buffer_rows, dtype=jnp.int32)[None, None, :]
    ).astype(jnp.float32)
    membership = jnp.sum(placed, axis=1)
    weighting = jnp.sum(placed * gates[:, :, None], axis=1)
    quarter = tokens.shape[1]
    rows = jnp.einsum(
        "tr,td->rd", membership.astype(jnp.bfloat16), tokens, preferred_element_type=jnp.float32
    ).astype(jnp.bfloat16)
    scaled = jnp.einsum(
        "tr,td->rd", weighting, cotangent.astype(jnp.float32), precision=highest
    ).astype(jnp.bfloat16)
    send = jnp.concatenate(
        [
            rows.reshape(devices, local_experts, capacity, quarter),
            scaled.reshape(devices, local_experts, capacity, quarter),
        ],
        axis=2,
    )
    arrived = lax.all_to_all(send, "expert", split_axis=0, concat_axis=0, tiled=True)
    whole = lax.all_gather(arrived, "tensor", axis=3, tiled=True)
    expert_rows = whole[:, :, :capacity]
    expert_scaled = whole[:, :, capacity:]
    preact = jnp.einsum("nesd,edh->nesh", expert_rows, w_in, preferred_element_type=jnp.float32)
    sigmoid_val = jax.nn.sigmoid(preact)
    hidden = (preact * sigmoid_val).astype(jnp.bfloat16)
    out_part = jnp.einsum("nesh,ehd->nesd", hidden, w_out, preferred_element_type=jnp.float32)
    grad_hidden = jnp.einsum(
        "nesd,ehd->nesh", expert_scaled, w_out, preferred_element_type=jnp.float32
    )
    grad_preact = (grad_hidden * sigmoid_val * (1.0 + preact * (1.0 - sigmoid_val))).astype(
        jnp.bfloat16
    )
    d_w_out = jnp.einsum(
        "nesh,nesd->ehd", hidden, expert_scaled, preferred_element_type=jnp.float32
    ).astype(jnp.bfloat16)
    d_w_in = jnp.einsum(
        "nesd,nesh->edh", expert_rows, grad_preact, preferred_element_type=jnp.float32
    ).astype(jnp.bfloat16)
    grad_part = jnp.einsum("nesh,edh->nesd", grad_preact, w_in, preferred_element_type=jnp.float32)
    parts = jnp.concatenate([out_part.astype(jnp.bfloat16), grad_part.astype(jnp.bfloat16)], axis=2)
    sums = lax.psum_scatter(parts, "tensor", scatter_dimension=3, tiled=True)
    back = lax.all_to_all(sums, "expert", split_axis=0, concat_axis=0, tiled=True)
    back_out = back[:, :, :capacity].reshape(buffer_rows, quarter).astype(jnp.float32)
    back_grad = back[:, :, capacity:].reshape(buffer_rows, quarter).astype(jnp.float32)
    mixed = jnp.einsum("tr,rd->td", weighting, back_out, precision=highest).astype(jnp.bfloat16)
    d_tokens = jnp.einsum("tr,rd->td", membership, back_grad, precision=highest).astype(
        jnp.bfloat16
    )
    return (mixed, d_tokens, d_w_in, d_w_out)


def solution(mesh):
    placed = (
        P("expert", "tensor"),
        P("expert", "tensor"),
        P("expert", None),
        P("expert", None),
        P("expert", None, "tensor"),
        P("expert", "tensor", None),
    )
    return jax.shard_map(
        shards,
        mesh=mesh,
        in_specs=placed,
        out_specs=(
            P("expert", "tensor"),
            P("expert", "tensor"),
            P("expert", None, "tensor"),
            P("expert", "tensor", None),
        ),
        check_vma=False,
    )
```

profile of v0, /device:TPU:2, one launch (start us, length us, event | category | flops | bytes accessed | tf_op | source)
XLA Modules:
  0.0 343.1 jit_solution(5815221899172722763)
XLA Ops:
  7.2 0.8 bitcast_or_fusion
  8.1 0.8 copy.47
  9.1 0.8 copy.51
  10.0 1.9 gather_fusion
  12.2 0.4 convert_reduce_fusion
  12.6 0.5 fusion.10
  13.1 1.0 fusion.11
  14.1 0.2 pad_maximum_fusion.1
  14.4 63.2 %all_to_all.10 = bf16[64,1,16,1024]{3,2,1,0:T(8,128)(2,1)} all-to-all(bf16[64,1,16,1024]{3,2,1,0:T(8,128)(2,1)S(1)} %pad_maximum_fusion.1), channel_id=1, replica_groups=mesh['expert'=64,'tensor'=4] {'expert'}, dimensions={0} | all-to-all | bytes 4194304 | tf_op jit(solution)/shard_map/all_to_all | solution.py:40
  77.6 0.2 reduce-scatter.2.cloned.1.call-start
  77.8 82.0 %all-gather.2.cloned.1.call-done = bf16[64,1,16,4096]{3,2,0,1:T(8,128)(2,1)} async-done(((bf16[64,1,16,1024]{3,2,0,1:T(8,128)(2,1)}), bf16[64,1,16,4096]{3,2,0,1:T(8,128)(2,1)}) %all-gather.2.cloned.1.call-update) | async-done | bytes 8388624 | tf_op jit(solution)/shard_map/all_gather | solution.py:41
  159.8 5.5 %fusion.18 = f32[64,1,8,384]{3,2,0,1:T(8,128)S(1)} fusion(bf16[1,4096,384]{2,1,0:T(8,128)(2,1)} %param.10, bf16[64,1,16,4096]{3,2,0,1:T(8,128)(2,1)} %all-gather.2.cloned.1.call-done), kind=kOutput, calls=%fused_computation.25 | convolution fusion | flops 1610612736 | bytes 8126464 | tf_op jit(solution)/shard_map/nesd,edh->nesh/dot_general | solution.py:44
  165.3 4.3 %fusion = bf16[64,1,8,4096]{3,2,0,1:T(8,128)(2,1)} fusion(bf16[1,384,4096]{2,1,0:T(8,128)(2,1)S(1)} %copy-done, f32[64,1,8,384]{3,2,0,1:T(8,128)S(1)} %fusion.18), kind=kOutput, calls=%fused_computation.6 | convolution fusion | flops 1613692928 | bytes 8126464 | tf_op jit(solution)/shard_map/nesh,ehd->nesd/dot_general | solution.py:47
  169.8 2.4 fusion.27
  172.2 0.8 copy-done.6
  173.0 4.3 %fusion.1 = bf16[64,1,8,4096]{3,2,0,1:T(8,128)(2,1)} fusion(bf16[64,8,384]{2,1,0:T(8,128)(2,1)S(1)} %fusion.27, bf16[1,4096,384]{2,1,0:T(8,128)(2,1)S(1)} %copy-done.5), kind=kOutput, calls=%fused_computation.7 | convolution fusion | flops 1612709888 | bytes 7733248 | tf_op jit(solution)/shard_map/nesh,edh->nesd/dot_general | solution.py:60
  177.4 7.8 %pad_maximum_fusion = bf16[64,1,16,4096]{3,2,0,1:T(8,128)(2,1)} fusion(bf16[64,1,8,4096]{3,2,0,1:T(8,128)(2,1)} %fusion.1, bf16[64,1,8,4096]{3,2,0,1:T(8,128)(2,1)} %fusion), kind=kLoop, calls=%fused_computation.1 | loop fusion | flops 16777216 | bytes 16777216 | tf_op jit(solution)/shard_map/concatenate | solution.py:61
  185.2 6.0 %fusion.3 = bf16[1,384,4096]{2,1,0:T(8,128)(2,1)} fusion(bf16[64,1,16,4096]{3,2,0,1:T(8,128)(2,1)} %all-gather.2.cloned.1.call-done, f32[64,1,8,384]{3,2,0,1:T(8,128)} %copy-done.7), kind=kOutput, calls=%fused_computation.9 | convolution fusion | flops 1613168640 | bytes 8126464 | tf_op jit(solution)/shard_map/nesh,nesd->ehd/dot_general | solution.py:54
  191.2 78.3 %reduce-scatter.2.cloned.1.call-done = bf16[64,1,16,1024]{3,2,0,1:T(8,128)(2,1)} async-done(((bf16[64,1,16,4096]{3,2,0,1:T(8,128)(2,1)}), bf16[64,1,16,1024]{3,2,0,1:T(8,128)(2,1)}) %reduce-scatter.2.cloned.1.call-update) | async-done | bytes 2097168 | tf_op jit(solution)/shard_map/reduce_scatter | solution.py:62
  269.4 10.7 %all-to-all-start.1 = ((bf16[64,1,16,1024]{3,2,1,0:T(8,128)(2,1)}), bf16[64,1,16,1024]{3,2,1,0:T(8,128)(2,1)}, u32[]{:S(2)}, u32[]{:S(2)}) async-start(bf16[64,1,16,1024]{3,2,1,0:T(8,128)(2,1)} %bitcast.123), calls=%async_computation.2 | async-start | bytes 4194304 | tf_op jit(solution)/shard_map/all_to_all | solution.py:63
  280.2 6.3 %fusion.2 = bf16[1,4096,384]{2,1,0:T(8,128)(2,1)} fusion(bf16[64,8,384]{2,1,0:T(8,128)(2,1)} %copy-done.6, bf16[64,1,16,4096]{3,2,0,1:T(8,128)(2,1)} %all-gather.2.cloned.1.call-done), kind=kOutput, calls=%fused_computation.8 | convolution fusion | flops 1612185600 | bytes 7733248 | tf_op jit(solution)/shard_map/nesd,nesh->edh/dot_general | solution.py:57
  286.5 44.9 %all-to-all-done.1 = bf16[64,1,16,1024]{3,2,1,0:T(8,128)(2,1)} async-done(((bf16[64,1,16,1024]{3,2,1,0:T(8,128)(2,1)}), bf16[64,1,16,1024]{3,2,1,0:T(8,128)(2,1)}, u32[]{:S(2)}, u32[]{:S(2)}) %all-to-all-start.1) | async-done | bytes 2097184 | tf_op jit(solution)/shard_map/all_to_all | solution.py:63
  331.3 2.5 convolution_convert_fusion.4
  333.8 2.5 convolution_convert_fusion.5
  (27 shorter events, 0.8 us)
Async XLA Ops:
  7.2 158.1 %copy-start = (bf16[1,384,4096]{2,1,0:T(8,128)(2,1)S(1)}, bf16[1,384,4096]{2,1,0:T(8,128)(2,1)}, u32[]{:S(2)}) copy-start(bf16[1,384,4096]{2,1,0:T(8,128)(2,1)} %param.11) | copy-start | bytes 9437188
  7.2 152.6 %all-gather.2.cloned.1.call-start = ((), (), s32[]{:S(2)}) async-start(), calls=%async_computation.3 | async-start | bytes 10485760 | tf_op jit(solution)/shard_map/all_gather | solution.py:41
  10.0 2.1 copy-start.3
  10.0 2.6 copy-start.1
  10.0 3.1 copy-start.2
  77.6 191.8 %reduce-scatter.2.cloned.1.call-start = ((), (), s32[]{:S(2)}) async-start(), calls=%async_computation.4 | async-start | bytes 10485760 | tf_op jit(solution)/shard_map/reduce_scatter | solution.py:62
  165.3 4.3 %copy-start.7 = (f32[64,1,8,384]{3,2,0,1:T(8,128)}, f32[64,1,8,384]{3,2,0,1:T(8,128)S(1)}, u32[]{:S(2)}) copy-start(f32[64,1,8,384]{3,2,0,1:T(8,128)S(1)} %fusion.18) | copy-start | bytes 2359300
  165.3 4.4 %copy-start.4 = (bf16[64,1,16,4096]{3,2,0,1:T(8,128)(2,1)S(1)}, bf16[64,1,16,4096]{3,2,0,1:T(8,128)(2,1)}, u32[]{:S(2)}) copy-start(bf16[64,1,16,4096]{3,2,0,1:T(8,128)(2,1)} %all-gather.2.cloned.1.call-done) | copy-start | bytes 25165828
  169.7 3.3 copy-start.5
  172.2 0.8 copy-start.6
  269.4 61.9 %all-to-all-start.1 = ((bf16[64,1,16,1024]{3,2,1,0:T(8,128)(2,1)}), bf16[64,1,16,1024]{3,2,1,0:T(8,128)(2,1)}, u32[]{:S(2)}, u32[]{:S(2)}) async-start(bf16[64,1,16,1024]{3,2,1,0:T(8,128)(2,1)} %bitcast.123), calls=%async_computation.2 | async-start | bytes 4194304 | tf_op jit(solution)/shard_map/all_to_all | solution.py:63
Sparse Core Ops, SparseCore 0:
  77.7 82.0 all-gather.1
  185.3 84.0 reduce-scatter.1
where the time goes:
time: 343 us
  waiting for transfers between devices  205 us (60%)
  blocking collectives  63.2 us (18%)
  matrix products  35.2 us (10%)
  between operations  14.2 us (4%)
  starting transfers between devices  11 us (3%)
  other arithmetic  9.46 us (3%)
  local copies, waits for them, and re-layouts  4.91 us (1%)
    all_gather x1, waiting for transfers between devices, shards(): whole = lax.all_gather(arrived, 'tensor', axis=3, tiled=True)  82 us
    reduce_scatter x1, waiting for transfers between devices, shards(): sums = lax.psum_scatter(parts, 'tensor', scatter_dimension=3, tiled=True)  78.3 us
    all_to_all x1, blocking collectives, shards(): lax.all_to_all(send, 'expert', split_axis=0, concat_axis=0, tiled=True)  63.2 us
    all_to_all x1, waiting for transfers between devices, shards(): lax.all_to_all(sums, 'expert', split_axis=0, concat_axis=0, tiled=True)  44.9 us
    all_to_all x1, starting transfers between devices, shards(): lax.all_to_all(sums, 'expert', split_axis=0, concat_axis=0, tiled=True)  10.7 us
    concatenate x1, other arithmetic, shards(): jnp.concatenate([out_part.astype(jnp.bfloat16), grad_part.astype(jnp.bflo...  7.8 us
  transfers between devices with their start and end apart: 3, of which 3 were waited for; matrix products, arithmetic and copies ran while one was open for 4% of the time, Pallas kernels for 0%

commit v1 on v0

--- a/solution.py
+++ b/solution.py
@@ -2,6 +2,13 @@
 import jax.numpy as jnp
 from jax import lax
 from jax.sharding import PartitionSpec as P
+
+
+def all_by_exchange(x, axis, d):
+    size = lax.axis_size(axis)
+    tiles = jnp.stack([x for _ in range(size)])
+    tiles = lax.all_to_all(tiles, axis, split_axis=0, concat_axis=0)
+    return jnp.concatenate(tiles, axis=d)
 
 
 def shards(tokens, cotangent, routing, gates, w_in, w_out):
@@ -38,7 +45,7 @@
         axis=2,
     )
     arrived = lax.all_to_all(send, "expert", split_axis=0, concat_axis=0, tiled=True)
-    whole = lax.all_gather(arrived, "tensor", axis=3, tiled=True)
+    whole = all_by_exchange(arrived, "tensor", 3)
     expert_rows = whole[:, :, :capacity]
     expert_scaled = whole[:, :, capacity:]
     preact = jnp.einsum("nesd,edh->nesh", expert_rows, w_in, preferred_element_type=jnp.float32)

time: 343 us -> 360 us (1.050)
  blocking collectives: 63.2 us -> 160 us
  waiting for transfers between devices: 205 us -> 118 us
  local copies, waits for them, and re-layouts: 4.91 us -> 13.2 us
    all_to_all x0 -> x1, blocking collectives: none -> 96.7 us  [all_by_exchange(): tiles = lax.all_to_all(tiles, axis, split_axis=0, concat_axis=0)]
    all_gather x1 -> x0, waiting for transfers between devices: 82 us -> none  [shards(): whole = lax.all_gather(arrived, 'tensor', axis=3, tiled=True)]
    reshape x0 -> x1, local copies, waits for them, and re-layouts: none -> 8.18 us  [all_by_exchange(): return jnp.concatenate(tiles, axis=d)]
    reduce_scatter x1, waiting for transfers between devices: 78.3 us -> 73 us  [shards(): sums = lax.psum_scatter(parts, 'tensor', scatter_dimension=3, tiled=True)]
  transfers between devices with their start and end apart: 3 -> 2, of which waited for: 3 -> 2; matrix products, arithmetic and copies ran while one was open for 4% -> 3% of each run, Pallas kernels for 0% -> 0%
where the time goes in v1:
time: 360 us
  blocking collectives  160 us (44%)
  waiting for transfers between devices  118 us (33%)
  matrix products  34.4 us (10%)
  between operations  14.2 us (4%)
  local copies, waits for them, and re-layouts  13.2 us (4%)
  starting transfers between devices  11 us (3%)
  other arithmetic  9.44 us (3%)
    all_to_all x1, blocking collectives, all_by_exchange(): tiles = lax.all_to_all(tiles, axis, split_axis=0, concat_axis=0)  96.7 us
    reduce_scatter x1, waiting for transfers between devices, shards(): sums = lax.psum_scatter(parts, 'tensor', scatter_dimension=3, tiled=True)  73 us
    all_to_all x1, blocking collectives, shards(): lax.all_to_all(send, 'expert', split_axis=0, concat_axis=0, tiled=True)  63.1 us
    all_to_all x1, waiting for transfers between devices, shards(): lax.all_to_all(sums, 'expert', split_axis=0, concat_axis=0, tiled=True)  44.9 us
    all_to_all x1, starting transfers between devices, shards(): lax.all_to_all(sums, 'expert', split_axis=0, concat_axis=0, tiled=True)  10.9 us
    reshape x1, local copies, waits for them, and re-layouts, all_by_exchange(): return jnp.concatenate(tiles, axis=d)  8.18 us
    concatenate x1, other arithmetic, shards(): jnp.concatenate([out_part.astype(jnp.bfloat16), grad_part.astype(jnp.bflo...  7.78 us
  transfers between devices with their start and end apart: 2, of which 2 were waited for; matrix products, arithmetic and copies ran while one was open for 3% of the time, Pallas kernels for 0%

profile of v1, /device:TPU:2, one launch (start us, length us, event | category | flops | bytes accessed | tf_op | source)
XLA Modules:
  0.0 359.9 jit_solution(3631885361740682616)
XLA Ops:
  7.2 0.8 bitcast_or_fusion
  8.1 0.8 copy.47
  9.1 0.8 copy.51
  10.0 1.9 gather_fusion
  12.2 0.4 convert_reduce_fusion
  12.6 0.5 fusion.10
  13.1 1.0 fusion.11
  14.1 0.2 pad_maximum_fusion.1
  14.4 63.1 %all_to_all.18 = bf16[64,1,16,1024]{3,2,1,0:T(8,128)(2,1)S(1)} all-to-all(bf16[64,1,16,1024]{3,2,1,0:T(8,128)(2,1)S(1)} %pad_maximum_fusion.1), channel_id=1, replica_groups=mesh['expert'=64,'tensor'=4] {'expert'}, dimensions={0} | all-to-all | bytes 4194304 | tf_op jit(solution)/shard_map/all_to_all | solution.py:47
  77.5 1.1 stack.2
  78.6 96.7 %all_to_all.19 = bf16[4,64,1,16,1024]{4,3,1,2,0:T(8,128)(2,1)} all-to-all(bf16[4,64,1,16,1024]{4,3,1,2,0:T(8,128)(2,1)S(1)} %stack.2), channel_id=1, replica_groups=mesh['expert'=64,'tensor'=4] {'tensor'}, dimensions={0} | all-to-all | bytes 16777216 | tf_op jit(solution)/shard_map/all_to_all | solution.py:10
  175.3 8.2 %copy.56 = bf16[4,1,64,2,8,1024]{5,4,0,3,2,1:T(8,128)(2,1)} copy(bf16[4,1,64,2,8,1024]{5,4,3,2,1,0:T(8,128)(2,1)} %bitcast.125) | data formatting | bytes 16777216 | tf_op jit(solution)/shard_map/reshape | solution.py:11
  183.5 4.7 %fusion.18 = f32[64,1,8,384]{3,2,0,1:T(8,128)S(1)} fusion(bf16[1,4096,384]{2,1,0:T(8,128)(2,1)S(1)} %copy-done.5, bf16[64,1,16,4096]{3,2,0,1:T(8,128)(2,1)} %bitcast.127), kind=kOutput, calls=%fused_computation.25 | convolution fusion | flops 1610612736 | bytes 8126464 | tf_op jit(solution)/shard_map/nesd,edh->nesh/dot_general | solution.py:51
  188.2 2.4 fusion.27
  190.6 4.3 %fusion = bf16[64,1,8,4096]{3,2,0,1:T(8,128)(2,1)} fusion(bf16[1,384,4096]{2,1,0:T(8,128)(2,1)S(1)} %copy-done, f32[64,1,8,384]{3,2,0,1:T(8,128)S(1)} %fusion.18), kind=kOutput, calls=%fused_computation.6 | convolution fusion | flops 1613692928 | bytes 8126464 | tf_op jit(solution)/shard_map/nesh,ehd->nesd/dot_general | solution.py:54
  194.9 4.3 %fusion.1 = bf16[64,1,8,4096]{3,2,0,1:T(8,128)(2,1)} fusion(bf16[64,8,384]{2,1,0:T(8,128)(2,1)S(1)} %fusion.27, bf16[1,4096,384]{2,1,0:T(8,128)(2,1)S(1)} %copy-done.5), kind=kOutput, calls=%fused_computation.7 | convolution fusion | flops 1612709888 | bytes 7733248 | tf_op jit(solution)/shard_map/nesh,edh->nesd/dot_general | solution.py:67
  199.2 7.8 %pad_maximum_fusion = bf16[64,1,16,4096]{3,2,0,1:T(8,128)(2,1)} fusion(bf16[64,1,8,4096]{3,2,0,1:T(8,128)(2,1)} %fusion.1, bf16[64,1,8,4096]{3,2,0,1:T(8,128)(2,1)} %fusion), kind=kLoop, calls=%fused_computation.1 | loop fusion | flops 16777216 | bytes 16777216 | tf_op jit(solution)/shard_map/concatenate | solution.py:68
  207.1 6.0 %fusion.3 = bf16[1,384,4096]{2,1,0:T(8,128)(2,1)} fusion(bf16[64,1,16,4096]{3,2,0,1:T(8,128)(2,1)} %bitcast.128, f32[64,1,8,384]{3,2,0,1:T(8,128)} %copy-done.7), kind=kOutput, calls=%fused_computation.9 | convolution fusion | flops 1613168640 | bytes 8126464 | tf_op jit(solution)/shard_map/nesh,nesd->ehd/dot_general | solution.py:61
  213.0 73.0 %reduce-scatter.2.cloned.1.call-done = bf16[64,1,16,1024]{3,2,0,1:T(8,128)(2,1)} async-done(((bf16[64,1,16,4096]{3,2,0,1:T(8,128)(2,1)}), bf16[64,1,16,1024]{3,2,0,1:T(8,128)(2,1)}) %reduce-scatter.2.cloned.1.call-update) | async-done | bytes 2097168 | tf_op jit(solution)/shard_map/reduce_scatter | solution.py:69
  286.0 10.9 %all-to-all-start.2 = ((bf16[64,1,16,1024]{3,2,1,0:T(8,128)(2,1)}), bf16[64,1,16,1024]{3,2,1,0:T(8,128)(2,1)}, u32[]{:S(2)}, u32[]{:S(2)}) async-start(bf16[64,1,16,1024]{3,2,1,0:T(8,128)(2,1)} %bitcast.131), calls=%async_computation.3 | async-start | bytes 4194304 | tf_op jit(solution)/shard_map/all_to_all | solution.py:70
  297.0 6.3 %fusion.2 = bf16[1,4096,384]{2,1,0:T(8,128)(2,1)} fusion(bf16[64,8,384]{2,1,0:T(8,128)(2,1)} %copy-done.6, bf16[64,1,16,4096]{3,2,0,1:T(8,128)(2,1)} %bitcast.129), kind=kOutput, calls=%fused_computation.8 | convolution fusion | flops 1612185600 | bytes 7733248 | tf_op jit(solution)/shard_map/nesd,nesh->edh/dot_general | solution.py:64
  303.3 44.9 %all-to-all-done.2 = bf16[64,1,16,1024]{3,2,1,0:T(8,128)(2,1)} async-done(((bf16[64,1,16,1024]{3,2,1,0:T(8,128)(2,1)}), bf16[64,1,16,1024]{3,2,1,0:T(8,128)(2,1)}, u32[]{:S(2)}, u32[]{:S(2)}) %all-to-all-start.2) | async-done | bytes 2097184 | tf_op jit(solution)/shard_map/all_to_all | solution.py:70
  348.2 2.5 convolution_convert_fusion.4
  350.6 2.5 convolution_convert_fusion.5
  (27 shorter events, 0.7 us)
Async XLA Ops:
  7.2 181.0 %copy-start = (bf16[1,384,4096]{2,1,0:T(8,128)(2,1)S(1)}, bf16[1,384,4096]{2,1,0:T(8,128)(2,1)}, u32[]{:S(2)}) copy-start(bf16[1,384,4096]{2,1,0:T(8,128)(2,1)} %param.11) | copy-start | bytes 9437188
  7.2 278.8 %reduce-scatter.2.cloned.1.call-start = ((), (), s32[]{:S(2)}) async-start(), calls=%async_computation.4 | async-start | bytes 10485760 | tf_op jit(solution)/shard_map/reduce_scatter | solution.py:69
  10.0 2.1 copy-start.4
  10.0 2.6 copy-start.2
  10.0 3.1 copy-start.3
  175.3 8.2 %copy-start.5 = (bf16[1,4096,384]{2,1,0:T(8,128)(2,1)S(1)}, bf16[1,4096,384]{2,1,0:T(8,128)(2,1)}, u32[]{:S(2)}) copy-start(bf16[1,4096,384]{2,1,0:T(8,128)(2,1)} %param.10) | copy-start | bytes 9437188
  183.5 4.7 %copy-start.1 = (bf16[4,1,64,2,8,1024]{5,4,0,3,2,1:T(8,128)(2,1)S(1)}, bf16[4,1,64,2,8,1024]{5,4,0,3,2,1:T(8,128)(2,1)}, u32[]{:S(2)}) copy-start(bf16[4,1,64,2,8,1024]{5,4,0,3,2,1:T(8,128)(2,1)} %copy.56) | copy-start | bytes 25165828
  188.2 2.5 copy-start.7
  190.6 4.3 %copy-start.6 = (bf16[64,8,384]{2,1,0:T(8,128)(2,1)}, bf16[64,8,384]{2,1,0:T(8,128)(2,1)S(1)}, u32[]{:S(2)}) copy-start(bf16[64,8,384]{2,1,0:T(8,128)(2,1)S(1)} %fusion.27) | copy-start | bytes 1179652
  286.0 62.1 %all-to-all-start.2 = ((bf16[64,1,16,1024]{3,2,1,0:T(8,128)(2,1)}), bf16[64,1,16,1024]{3,2,1,0:T(8,128)(2,1)}, u32[]{:S(2)}, u32[]{:S(2)}) async-start(bf16[64,1,16,1024]{3,2,1,0:T(8,128)(2,1)} %bitcast.131), calls=%async_computation.3 | async-start | bytes 4194304 | tf_op jit(solution)/shard_map/all_to_all | solution.py:70
Sparse Core Ops, SparseCore 0:
  207.2 78.7 reduce-scatter.1
